TPU v7x, 256 devices: a whole 4x4x8 slice. The times are simulated.
256 devices in a mesh: row: 16 (over z, core), col: 16 (over y, x).
Axes of the slice: x: 4, y: 4, z: 8, core: 2. Of those that a mesh axis runs over, the one named last changes fastest.
Arguments:
- rhs: float32 [24576, 12288], P('row', 'col'), may hold values from -6 to 6
- panels_l: float32 [4, 24576, 512], P(None, 'row', 'col'), may hold values from -0.25 to 0.25
- diag_inverse: float32 [4, 512, 512], P(None, None, 'col'), may hold values from -1.5 to 1.5, as said below
Outputs:
- solved_rhs: float32 [24576, 12288], P('row', 'col')
Inputs may be any that keep to these rules, and one draw needn't show every extreme that they name: `diag_inverse`: each tile is lower triangular with diagonal entries between 0.5 and 1.5.
All inputs are finite; a program needn't handle non-finite values.
Results may differ from a plain program's by a relative error of at most 0.00016.
Values sent between devices are 32-bit elements; how exact they have to be, the bound alone decides.
A program may use at most 128 MiB of HBM per device.

v0:
```python
import jax
import jax.numpy as jnp
from jax import lax
from jax.sharding import PartitionSpec as P


def spread(x, axis, root):
    mine = lax.axis_index(axis) == root
    return lax.psum(jnp.where(mine, x, jnp.zeros_like(x)), axis)


def exact_dot(left, right):
    return jnp.dot(left, right, precision=lax.Precision.HIGHEST, preferred_element_type=jnp.float32)


def per_device(rhs, panels_l, diag_inverse):
    rows_here = rhs.shape[0]
    width = diag_inverse.shape[1]
    count = panels_l.shape[0]
    my_row = lax.axis_index("row")
    global_rows = my_row * rows_here + lax.iota(jnp.int32, rows_here)
    work = rhs
    for k in range(count):
        factor_cols = lax.all_gather(panels_l[k], "col", axis=1, tiled=True)
        inverse_tile = lax.all_gather(diag_inverse[k], "col", axis=1, tiled=True)
        owner = k * width // rows_here
        offset = k * width - owner * rows_here
        strip = work[offset : offset + width]
        is_owner = my_row == owner
        solved_here = lax.cond(
            is_owner,
            lambda: exact_dot(inverse_tile, strip),
            lambda: jnp.zeros(strip.shape, jnp.float32),
        )
        solved = spread(solved_here, "row", owner)
        update = exact_dot(factor_cols, solved)
        below = (global_rows >= (k + 1) * width)[:, None]
        work = jnp.where(below, work - update, work)
        work = work.at[offset : offset + width].set(
            jnp.where(is_owner, solved, work[offset : offset + width])
        )
    return work


def solution(mesh):
    in_specs = (P("row", "col"), P(None, "row", "col"), P(None, None, "col"))
    out_specs = P("row", "col")
    return jax.shard_map(
        per_device, mesh=mesh, in_specs=in_specs, out_specs=out_specs, check_vma=False
    )
```

profile of v0, /device:TPU:1, one launch (start us, length us, event | category | flops | bytes accessed | tf_op | source)
XLA Modules:
  0.0 919.6 jit_solution(2855108133627082533)
XLA Ops:
  8.3 51.0 %all-gather.17.cloned.1.call-done = f32[1,512,512]{1,0,2:T(1,128)} async-done(((f32[1,512,32]{1,0,2:T(1,128)}), f32[1,512,512]{1,0,2:T(1,128)}) %all-gather.17.cloned.1.call-update) | async-done | bytes 1048592 | tf_op jit(solution)/shard_map/all_gather | solution.py:25
  65.6 6.0 copy.21
  71.7 105.5 %all-reduce.5.cloned.1.call-done = f32[512,768]{0,1:T(8,128)} async-done(((f32[512,768]{0,1:T(8,128)}), f32[512,768]{0,1:T(8,128)}) %all-reduce.5.cloned.1.call-update) | async-done | bytes 1572880 | tf_op jit(solution)/shard_map/psum | solution.py:9
  177.2 55.1 %all-gather.19.cloned.1.call-done = f32[1,1536,512]{1,2,0:T(8,128)} async-done(((f32[1,1536,32]{1,2,0:T(8,128)}), f32[1,1536,512]{1,2,0:T(8,128)}) %all-gather.19.cloned.1.call-update) | async-done | bytes 3145744 | tf_op jit(solution)/shard_map/all_gather | solution.py:24
  232.3 12.0 %subtract_select_fusion.3 = f32[1536,768]{0,1:T(8,128)} fusion(f32[1536,768]{0,1:T(8,128)} %copy.21, f32[512,768]{0,1:T(8,128)} %all-reduce.5.cloned.1.call-done, f32[1,1536,512]{1,2,0:T(8,128)} %all-gather.19.cloned.1.call-done, pred[1536]{0:T(1024)(128)(4,1)S(1)} %fusion.22), kind=kOutput, calls=%fused_computation.17 | convolution fusion | flops 7250116608 | bytes 14157312 | tf_op jit(solution)/shard_map/dot_general | solution.py:13
  244.3 2.9 fusion.21
  247.2 32.6 %all-gather.21.cloned.1.call-done = f32[1,512,512]{1,0,2:T(1,128)} async-done(((f32[1,512,32]{1,0,2:T(1,128)}), f32[1,512,512]{1,0,2:T(1,128)}) %all-gather.21.cloned.1.call-update) | async-done | bytes 1048592 | tf_op jit(solution)/shard_map/all_gather | solution.py:25
  283.1 52.3 %all-gather.23.cloned.1.call-done = f32[1,1536,512]{1,2,0:T(8,128)} async-done(((f32[1,1536,32]{1,2,0:T(8,128)}), f32[1,1536,512]{1,2,0:T(8,128)}) %all-gather.23.cloned.1.call-update) | async-done | bytes 3145744 | tf_op jit(solution)/shard_map/all_gather | solution.py:24
  335.5 115.4 %all-reduce.7.cloned.1.call-done = f32[512,768]{0,1:T(8,128)} async-done(((f32[512,768]{0,1:T(8,128)}), f32[512,768]{0,1:T(8,128)}) %all-reduce.7.cloned.1.call-update) | async-done | bytes 1572880 | tf_op jit(solution)/shard_map/psum | solution.py:9
  450.9 12.9 %subtract_select_fusion.2 = f32[1536,768]{0,1:T(8,128)} fusion(f32[1536,768]{0,1:T(8,128)} %fusion.21, f32[512,768]{0,1:T(8,128)} %all-reduce.7.cloned.1.call-done, f32[1,1536,512]{1,2,0:T(8,128)} %all-gather.23.cloned.1.call-done, pred[1536]{0:T(1024)(128)(4,1)S(1)} %fusion.23), kind=kOutput, calls=%fused_computation.16 | convolution fusion | flops 7250116608 | bytes 14157312 | tf_op jit(solution)/shard_map/dot_general | solution.py:13
  463.8 2.9 fusion.20
  466.7 32.8 %all-gather.25.cloned.1.call-done = f32[1,512,512]{1,0,2:T(1,128)} async-done(((f32[1,512,32]{1,0,2:T(1,128)}), f32[1,512,512]{1,0,2:T(1,128)}) %all-gather.25.cloned.1.call-update) | async-done | bytes 1048592 | tf_op jit(solution)/shard_map/all_gather | solution.py:25
  502.8 52.5 %all-gather.27.cloned.1.call-done = f32[1,1536,512]{1,2,0:T(8,128)} async-done(((f32[1,1536,32]{1,2,0:T(8,128)}), f32[1,1536,512]{1,2,0:T(8,128)}) %all-gather.27.cloned.1.call-update) | async-done | bytes 3145744 | tf_op jit(solution)/shard_map/all_gather | solution.py:24
  555.3 115.6 %all-reduce.9.cloned.1.call-done = f32[512,768]{0,1:T(8,128)} async-done(((f32[512,768]{0,1:T(8,128)}), f32[512,768]{0,1:T(8,128)}) %all-reduce.9.cloned.1.call-update) | async-done | bytes 1572880 | tf_op jit(solution)/shard_map/psum | solution.py:9
  670.9 12.9 %subtract_select_fusion.1 = f32[1536,768]{0,1:T(8,128)} fusion(f32[1536,768]{0,1:T(8,128)} %fusion.20, f32[512,768]{0,1:T(8,128)} %all-reduce.9.cloned.1.call-done, f32[1,1536,512]{1,2,0:T(8,128)} %all-gather.27.cloned.1.call-done, pred[1536]{0:T(1024)(128)(4,1)S(1)} %fusion.24), kind=kOutput, calls=%fused_computation.15 | convolution fusion | flops 7250116608 | bytes 14157312 | tf_op jit(solution)/shard_map/dot_general | solution.py:13
  686.7 32.7 %all-gather.29.cloned.1.call-done = f32[1,512,512]{1,0,2:T(1,128)} async-done(((f32[1,512,32]{1,0,2:T(1,128)}), f32[1,512,512]{1,0,2:T(1,128)}) %all-gather.29.cloned.1.call-update) | async-done | bytes 1048592 | tf_op jit(solution)/shard_map/all_gather | solution.py:25
  719.4 10.5 %conditional.7 = (f32[512,768]{0,1:T(8,128)S(1)}) conditional(s32[]{:T(128)} %convert_element_type.9, () %tuple.51, (f32[1536,768]{0,1:T(8,128)}, f32[1,512,512]{1,0,2:T(1,128)}) %tuple.52), branch_computations={%region_9.10_spmd, %region_10.11_spmd} | conditional | flops 2415919104 | bytes 17825828 | solution.py:30
  719.4 6.1 copy.32
  725.5 4.1 fusion.10
  731.2 44.0 %all-gather.31.cloned.1.call-done = f32[1,1536,512]{1,2,0:T(8,128)} async-done(((f32[1,1536,32]{1,2,0:T(8,128)}), f32[1,1536,512]{1,2,0:T(8,128)}) %all-gather.31.cloned.1.call-update) | async-done | bytes 3145744 | tf_op jit(solution)/shard_map/all_gather | solution.py:24
  775.2 115.4 %all-reduce.11.cloned.1.call-done = f32[512,768]{0,1:T(8,128)} async-done(((f32[512,768]{0,1:T(8,128)}), f32[512,768]{0,1:T(8,128)}) %all-reduce.11.cloned.1.call-update) | async-done | bytes 1572880 | tf_op jit(solution)/shard_map/psum | solution.py:9
  890.6 13.1 %subtract_select_fusion = f32[1536,768]{0,1:T(8,128)} fusion(f32[1536,768]{0,1:T(8,128)} %fusion.19, f32[512,768]{0,1:T(8,128)} %all-reduce.11.cloned.1.call-done, f32[1,1536,512]{1,2,0:T(8,128)} %all-gather.31.cloned.1.call-done, pred[1536]{0:T(1024)(128)(4,1)S(1)} %fusion.25), kind=kOutput, calls=%fused_computation.14 | convolution fusion | flops 7250116608 | bytes 14157312 | tf_op jit(solution)/shard_map/dot_general | solution.py:13
  903.6 3.0 fusion.18
  906.7 6.0 copy.35
  (58 shorter events, 19.3 us)
Async XLA Ops:
  6.5 52.8 %all-gather.17.cloned.1.call-start = ((), (), s32[]{:S(2)}) async-start(), calls=%async_computation.4 | async-start | bytes 1114112 | tf_op jit(solution)/shard_map/all_gather | solution.py:25
  8.2 169.0 %all-reduce.5.cloned.1.call-start = ((), (), s32[]{:S(2)}) async-start(), calls=%async_computation | async-start | bytes 3145728 | tf_op jit(solution)/shard_map/psum | solution.py:9
  62.2 1.1 copy-start.7
  62.2 170.2 %all-gather.19.cloned.1.call-start = ((), (), s32[]{:S(2)}) async-start(), calls=%async_computation.5 | async-start | bytes 3342336 | tf_op jit(solution)/shard_map/all_gather | solution.py:24
  64.2 215.6 %all-gather.21.cloned.1.call-start = ((), (), s32[]{:S(2)}) async-start(), calls=%async_computation.6 | async-start | bytes 1114112 | tf_op jit(solution)/shard_map/all_gather | solution.py:25
  65.0 270.5 %all-gather.23.cloned.1.call-start = ((), (), s32[]{:S(2)}) async-start(), calls=%async_computation.7 | async-start | bytes 3342336 | tf_op jit(solution)/shard_map/all_gather | solution.py:24
  65.6 385.3 %all-reduce.7.cloned.1.call-start = ((), (), s32[]{:S(2)}) async-start(), calls=%async_computation.1 | async-start | bytes 3145728 | tf_op jit(solution)/shard_map/psum | solution.py:9
  177.2 67.1 %copy-start = (f32[512,768]{0,1:T(8,128)S(1)}, f32[512,768]{0,1:T(8,128)}, u32[]{:S(2)}) copy-start(f32[512,768]{0,1:T(8,128)} %all-reduce.5.cloned.1.call-done) | copy-start | bytes 4718596
  281.5 218.0 %all-gather.25.cloned.1.call-start = ((), (), s32[]{:S(2)}) async-start(), calls=%async_computation.8 | async-start | bytes 1114112 | tf_op jit(solution)/shard_map/all_gather | solution.py:25
  282.3 273.0 %all-gather.27.cloned.1.call-start = ((), (), s32[]{:S(2)}) async-start(), calls=%async_computation.9 | async-start | bytes 3342336 | tf_op jit(solution)/shard_map/all_gather | solution.py:24
  283.0 387.8 %all-reduce.9.cloned.1.call-start = ((), (), s32[]{:S(2)}) async-start(), calls=%async_computation.2 | async-start | bytes 3145728 | tf_op jit(solution)/shard_map/psum | solution.py:9
  450.9 12.9 %copy-start.2 = (f32[512,768]{0,1:T(8,128)S(1)}, f32[512,768]{0,1:T(8,128)}, u32[]{:S(2)}) copy-start(f32[512,768]{0,1:T(8,128)} %all-reduce.7.cloned.1.call-done) | copy-start | bytes 4718596
  501.1 218.3 %all-gather.29.cloned.1.call-start = ((), (), s32[]{:S(2)}) async-start(), calls=%async_computation.10 | async-start | bytes 1114112 | tf_op jit(solution)/shard_map/all_gather | solution.py:25
  501.8 273.4 %all-gather.31.cloned.1.call-start = ((), (), s32[]{:S(2)}) async-start(), calls=%async_computation.11 | async-start | bytes 3342336 | tf_op jit(solution)/shard_map/all_gather | solution.py:24
  502.6 388.0 %all-reduce.11.cloned.1.call-start = ((), (), s32[]{:S(2)}) async-start(), calls=%async_computation.3 | async-start | bytes 3145728 | tf_op jit(solution)/shard_map/psum | solution.py:9
  670.9 12.9 %copy-start.1 = (f32[512,768]{0,1:T(8,128)S(1)}, f32[512,768]{0,1:T(8,128)}, u32[]{:S(2)}) copy-start(f32[512,768]{0,1:T(8,128)} %all-reduce.9.cloned.1.call-done) | copy-start | bytes 4718596
  719.4 6.1 copy-start.4
  890.6 13.1 %copy-start.3 = (f32[512,768]{0,1:T(8,128)S(1)}, f32[512,768]{0,1:T(8,128)}, u32[]{:S(2)}) copy-start(f32[512,768]{0,1:T(8,128)} %all-reduce.11.cloned.1.call-done) | copy-start | bytes 4718596
Sparse Core Ops, SparseCore 0:
  9.8 49.4 all-gather.16
  62.3 114.8 all-reduce.4
  179.7 52.6 all-gather.18
  234.6 45.1 all-gather.20
  282.1 53.3 all-gather.22
  337.7 113.1 all-reduce.6
  453.3 46.1 all-gather.24
  501.9 53.3 all-gather.26
  557.7 113.1 all-reduce.8
  673.2 46.1 all-gather.28
  721.8 53.3 all-gather.30
  777.4 113.1 all-reduce.10
where the time goes:
time: 920 us
  waiting for transfers between devices  807 us (88%)
  matrix products  54.9 us (6%)
  local copies, waits for them, and re-layouts  25.7 us (3%)
  other arithmetic  17.1 us (2%)
  between operations  13.7 us (1%)
    psum x4, waiting for transfers between devices, spread(): return lax.psum(jnp.where(mine, x, jnp.zeros_like(x)), axis)  452 us
    all_gather x4, waiting for transfers between devices, per_device(): factor_cols = lax.all_gather(panels_l[k], 'col', axis=1, tiled=True)  204 us
    all_gather x4, waiting for transfers between devices, per_device(): inverse_tile = lax.all_gather(diag_inverse[k], 'col', axis=1, tiled=True)  149 us
    dot_general x4, matrix products, exact_dot(): jnp.dot(left, right, precision=lax.Precision.HIGHEST, preferred_element_t...  50.9 us
  transfers between devices with their start and end apart: 12, of which 12 were waited for; matrix products, arithmetic and copies ran while one was open for 8% of the time, Pallas kernels for 0%

commit v1 on v0

--- a/solution.py
+++ b/solution.py
@@ -4,9 +4,15 @@
 from jax.sharding import PartitionSpec as P
 
 
+def summed_here(block, axis):
+    terms = lax.all_gather(block, axis, axis=0, tiled=False)
+    total = terms.sum(axis=0)
+    return total
+
+
 def spread(x, axis, root):
     mine = lax.axis_index(axis) == root
-    return lax.psum(jnp.where(mine, x, jnp.zeros_like(x)), axis)
+    return summed_here(jnp.where(mine, x, jnp.zeros_like(x)), axis)
 
 
 def exact_dot(left, right):

time: 920 us -> 1010 us (1.098)
  local copies, waits for them, and re-layouts: 25.7 us -> 133 us
  waiting for transfers between devices: 807 us -> 767 us
  other arithmetic: 17.1 us -> 42.3 us
    all_gather x0 -> x4, waiting for transfers between devices: none -> 536 us  [summed_here(): terms = lax.all_gather(block, axis, axis=0, tiled=False)]
    psum x4 -> x0, waiting for transfers between devices: 452 us -> none  [spread(): return lax.psum(jnp.where(mine, x, jnp.zeros_like(x)), axis)]
    all_gather x4, waiting for transfers between devices: 204 us -> 78.7 us  [per_device(): factor_cols = lax.all_gather(panels_l[k], 'col', axis=1, tiled=True)]
    unnamed x16 -> x12, local copies, waits for them, and re-layouts: 11.2 us -> 118 us
    reduce_sum x0 -> x4, other arithmetic: none -> 25.2 us  [summed_here(): total = terms.sum(axis=0)]
  transfers between devices with their start and end apart: 12 -> 12, of which waited for: 12 -> 12; matrix products, arithmetic and copies ran while one was open for 8% -> 18% of each run, Pallas kernels for 0% -> 0%
where the time goes in v1:
time: 1010 us
  waiting for transfers between devices  767 us (76%)
  local copies, waits for them, and re-layouts  133 us (13%)
  matrix products  50.3 us (5%)
  other arithmetic  42.3 us (4%)
  between operations  13.9 us (1%)
    all_gather x4, waiting for transfers between devices, summed_here(): terms = lax.all_gather(block, axis, axis=0, tiled=False)  536 us
    all_gather x4, waiting for transfers between devices, per_device(): inverse_tile = lax.all_gather(diag_inverse[k], 'col', axis=1, tiled=True)  150 us
    unnamed x12, local copies, waits for them, and re-layouts  118 us
    all_gather x4, waiting for transfers between devices, per_device(): factor_cols = lax.all_gather(panels_l[k], 'col', axis=1, tiled=True)  78.7 us
    dot_general x4, matrix products, exact_dot(): jnp.dot(left, right, precision=lax.Precision.HIGHEST, preferred_element_t...  46.2 us
    reduce_sum x4, other arithmetic, summed_here(): total = terms.sum(axis=0)  25.2 us
  transfers between devices with their start and end apart: 12, of which 12 were waited for; matrix products, arithmetic and copies ran while one was open for 18% of the time, Pallas kernels for 0%

profile of v1, /device:TPU:1, one launch (start us, length us, event | category | flops | bytes accessed | tf_op | source)
XLA Modules:
  0.0 1007.2 jit_solution(10903538633584687298)
XLA Ops:
  8.3 51.0 %all-gather.25.cloned.1.call-done = f32[1,512,512]{1,0,2:T(1,128)} async-done(((f32[1,512,32]{1,0,2:T(1,128)}), f32[1,512,512]{1,0,2:T(1,128)}) %all-gather.25.cloned.1.call-update) | async-done | bytes 1048592 | tf_op jit(solution)/shard_map/all_gather | solution.py:31
  71.3 127.5 %all-gather.27.cloned.1.call-done = f32[8192,768]{0,1:T(8,128)} async-done(((f32[512,768]{0,1:T(8,128)}), f32[8192,768]{0,1:T(8,128)}) %all-gather.27.cloned.1.call-update) | async-done | bytes 25165840 | tf_op jit(solution)/shard_map/all_gather | solution.py:8
  198.8 26.7 %copy.56 = f32[96,8,16,512]{3,2,1,0:T(8,128)S(1)} copy(f32[96,8,16,512]{3,1,2,0:T(8,128)} %bitcast.57) | data formatting | bytes 50331648
  225.5 6.3 bitcast_reduce_fusion.3
  231.8 19.7 %all-gather.29.cloned.1.call-done = f32[1,1536,512]{1,2,0:T(8,128)} async-done(((f32[1,1536,32]{1,2,0:T(8,128)}), f32[1,1536,512]{1,2,0:T(8,128)}) %all-gather.29.cloned.1.call-update) | async-done | bytes 3145744 | tf_op jit(solution)/shard_map/all_gather | solution.py:30
  251.6 11.5 %subtract_select_fusion.3 = f32[1536,768]{0,1:T(8,128)} fusion(f32[1536,768]{0,1:T(8,128)} %copy.21, f32[512,768]{0,1:T(8,128)S(1)} %bitcast_reduce_fusion.3, f32[1,1536,512]{1,2,0:T(8,128)} %all-gather.29.cloned.1.call-done, pred[1536]{0:T(1024)(128)(4,1)S(1)} %fusion.22), kind=kOutput, calls=%fused_computation.21 | convolution fusion | flops 7250116608 | bytes 14157312 | tf_op jit(solution)/shard_map/dot_general | solution.py:19
  266.0 33.0 %all-gather.31.cloned.1.call-done = f32[1,512,512]{1,0,2:T(1,128)} async-done(((f32[1,512,32]{1,0,2:T(1,128)}), f32[1,512,512]{1,0,2:T(1,128)}) %all-gather.31.cloned.1.call-update) | async-done | bytes 1048592 | tf_op jit(solution)/shard_map/all_gather | solution.py:31
  302.4 140.1 %all-gather.33.cloned.1.call-done = f32[8192,768]{0,1:T(8,128)} async-done(((f32[512,768]{0,1:T(8,128)}), f32[8192,768]{0,1:T(8,128)}) %all-gather.33.cloned.1.call-update) | async-done | bytes 25165840 | tf_op jit(solution)/shard_map/all_gather | solution.py:8
  442.5 26.7 %copy.57 = f32[96,8,16,512]{3,2,1,0:T(8,128)S(1)} copy(f32[96,8,16,512]{3,1,2,0:T(8,128)} %bitcast.59) | data formatting | bytes 50331648
  469.2 6.3 bitcast_reduce_fusion.2
  475.5 19.6 %all-gather.35.cloned.1.call-done = f32[1,1536,512]{1,2,0:T(8,128)} async-done(((f32[1,1536,32]{1,2,0:T(8,128)}), f32[1,1536,512]{1,2,0:T(8,128)}) %all-gather.35.cloned.1.call-update) | async-done | bytes 3145744 | tf_op jit(solution)/shard_map/all_gather | solution.py:30
  495.1 11.5 %subtract_select_fusion.2 = f32[1536,768]{0,1:T(8,128)} fusion(f32[1536,768]{0,1:T(8,128)} %fusion.21, f32[512,768]{0,1:T(8,128)S(1)} %bitcast_reduce_fusion.2, f32[1,1536,512]{1,2,0:T(8,128)} %all-gather.35.cloned.1.call-done, pred[1536]{0:T(1024)(128)(4,1)S(1)} %fusion.23), kind=kOutput, calls=%fused_computation.20 | convolution fusion | flops 7250116608 | bytes 14157312 | tf_op jit(solution)/shard_map/dot_general | solution.py:19
  509.5 33.2 %all-gather.37.cloned.1.call-done = f32[1,512,512]{1,0,2:T(1,128)} async-done(((f32[1,512,32]{1,0,2:T(1,128)}), f32[1,512,512]{1,0,2:T(1,128)}) %all-gather.37.cloned.1.call-update) | async-done | bytes 1048592 | tf_op jit(solution)/shard_map/all_gather | solution.py:31
  546.1 139.9 %all-gather.39.cloned.1.call-done = f32[8192,768]{0,1:T(8,128)} async-done(((f32[512,768]{0,1:T(8,128)}), f32[8192,768]{0,1:T(8,128)}) %all-gather.39.cloned.1.call-update) | async-done | bytes 25165840 | tf_op jit(solution)/shard_map/all_gather | solution.py:8
  686.0 26.7 %copy.58 = f32[96,8,16,512]{3,2,1,0:T(8,128)S(1)} copy(f32[96,8,16,512]{3,1,2,0:T(8,128)} %bitcast.58) | data formatting | bytes 50331648
  712.7 6.3 bitcast_reduce_fusion.1
  719.0 19.7 %all-gather.41.cloned.1.call-done = f32[1,1536,512]{1,2,0:T(8,128)} async-done(((f32[1,1536,32]{1,2,0:T(8,128)}), f32[1,1536,512]{1,2,0:T(8,128)}) %all-gather.41.cloned.1.call-update) | async-done | bytes 3145744 | tf_op jit(solution)/shard_map/all_gather | solution.py:30
  738.7 11.5 %subtract_select_fusion.1 = f32[1536,768]{0,1:T(8,128)} fusion(f32[1536,768]{0,1:T(8,128)} %fusion.20, f32[512,768]{0,1:T(8,128)S(1)} %bitcast_reduce_fusion.1, f32[1,1536,512]{1,2,0:T(8,128)} %all-gather.41.cloned.1.call-done, pred[1536]{0:T(1024)(128)(4,1)S(1)} %fusion.24), kind=kOutput, calls=%fused_computation.19 | convolution fusion | flops 7250116608 | bytes 14157312 | tf_op jit(solution)/shard_map/dot_general | solution.py:19
  753.1 33.0 %all-gather.43.cloned.1.call-done = f32[1,512,512]{1,0,2:T(1,128)} async-done(((f32[1,512,32]{1,0,2:T(1,128)}), f32[1,512,512]{1,0,2:T(1,128)}) %all-gather.43.cloned.1.call-update) | async-done | bytes 1048592 | tf_op jit(solution)/shard_map/all_gather | solution.py:31
  786.2 10.4 %conditional.7 = (f32[512,768]{0,1:T(8,128)S(1)}) conditional(s32[]{:T(128)} %convert_element_type.9, () %tuple.51, (f32[1536,768]{0,1:T(8,128)}, f32[1,512,512]{1,0,2:T(1,128)}) %tuple.52), branch_computations={%region_9.10_spmd, %region_10.11_spmd} | conditional | flops 2415919104 | bytes 17825828 | solution.py:36
  798.6 128.3 %all-gather.45.cloned.1.call-done = f32[8192,768]{0,1:T(8,128)} async-done(((f32[512,768]{0,1:T(8,128)}), f32[8192,768]{0,1:T(8,128)}) %all-gather.45.cloned.1.call-update) | async-done | bytes 25165840 | tf_op jit(solution)/shard_map/all_gather | solution.py:8
  926.9 26.7 %copy.59 = f32[96,8,16,512]{3,2,1,0:T(8,128)S(1)} copy(f32[96,8,16,512]{3,1,2,0:T(8,128)} %bitcast.60) | data formatting | bytes 50331648
  959.9 19.6 %all-gather.47.cloned.1.call-done = f32[1,1536,512]{1,2,0:T(8,128)} async-done(((f32[1,1536,32]{1,2,0:T(8,128)}), f32[1,1536,512]{1,2,0:T(8,128)}) %all-gather.47.cloned.1.call-update) | async-done | bytes 3145744 | tf_op jit(solution)/shard_map/all_gather | solution.py:30
  979.5 11.6 %subtract_select_fusion = f32[1536,768]{0,1:T(8,128)} fusion(f32[1536,768]{0,1:T(8,128)} %fusion.19, f32[512,768]{0,1:T(8,128)S(1)} %bitcast_reduce_fusion, f32[1,1536,512]{1,2,0:T(8,128)} %all-gather.47.cloned.1.call-done, pred[1536]{0:T(1024)(128)(4,1)S(1)} %fusion.25), kind=kOutput, calls=%fused_computation.18 | convolution fusion | flops 7250116608 | bytes 14157312 | tf_op jit(solution)/shard_map/dot_general | solution.py:19
  (58 shorter events, 57.0 us)
Async XLA Ops:
  6.5 52.8 %all-gather.25.cloned.1.call-start = ((), (), s32[]{:S(2)}) async-start(), calls=%async_computation | async-start | bytes 1114112 | tf_op jit(solution)/shard_map/all_gather | solution.py:31
  8.2 190.6 %all-gather.27.cloned.1.call-start = ((), (), s32[]{:S(2)}) async-start(), calls=%async_computation.1 | async-start | bytes 26738688 | tf_op jit(solution)/shard_map/all_gather | solution.py:8
  62.2 1.1 copy-start.3
  62.2 189.4 %all-gather.29.cloned.1.call-start = ((), (), s32[]{:S(2)}) async-start(), calls=%async_computation.2 | async-start | bytes 3342336 | tf_op jit(solution)/shard_map/all_gather | solution.py:30
  64.2 234.8 %all-gather.31.cloned.1.call-start = ((), (), s32[]{:S(2)}) async-start(), calls=%async_computation.3 | async-start | bytes 1114112 | tf_op jit(solution)/shard_map/all_gather | solution.py:31
  65.0 377.5 %all-gather.33.cloned.1.call-start = ((), (), s32[]{:S(2)}) async-start(), calls=%async_computation.4 | async-start | bytes 26738688 | tf_op jit(solution)/shard_map/all_gather | solution.py:8
  301.0 194.1 %all-gather.35.cloned.1.call-start = ((), (), s32[]{:S(2)}) async-start(), calls=%async_computation.5 | async-start | bytes 3342336 | tf_op jit(solution)/shard_map/all_gather | solution.py:30
  301.6 241.1 %all-gather.37.cloned.1.call-start = ((), (), s32[]{:S(2)}) async-start(), calls=%async_computation.6 | async-start | bytes 1114112 | tf_op jit(solution)/shard_map/all_gather | solution.py:31
  302.4 383.6 %all-gather.39.cloned.1.call-start = ((), (), s32[]{:S(2)}) async-start(), calls=%async_computation.7 | async-start | bytes 26738688 | tf_op jit(solution)/shard_map/all_gather | solution.py:8
  544.5 194.2 %all-gather.41.cloned.1.call-start = ((), (), s32[]{:S(2)}) async-start(), calls=%async_computation.8 | async-start | bytes 3342336 | tf_op jit(solution)/shard_map/all_gather | solution.py:30
  545.2 241.0 %all-gather.43.cloned.1.call-start = ((), (), s32[]{:S(2)}) async-start(), calls=%async_computation.9 | async-start | bytes 1114112 | tf_op jit(solution)/shard_map/all_gather | solution.py:31
  546.0 380.9 %all-gather.45.cloned.1.call-start = ((), (), s32[]{:S(2)}) async-start(), calls=%async_computation.10 | async-start | bytes 26738688 | tf_op jit(solution)/shard_map/all_gather | solution.py:8
  786.4 6.1 copy-start
  798.0 181.5 %all-gather.47.cloned.1.call-start = ((), (), s32[]{:S(2)}) async-start(), calls=%async_computation.11 | async-start | bytes 3342336 | tf_op jit(solution)/shard_map/all_gather | solution.py:30
Sparse Core Ops, SparseCore 0:
  9.8 49.4 all-gather.24
  62.3 136.4 all-gather.26
  201.2 50.2 all-gather.28
  253.9 45.1 all-gather.30
  301.2 141.2 all-gather.32
  444.8 50.2 all-gather.34
  497.5 45.1 all-gather.36
  544.6 141.2 all-gather.38
  688.4 50.2 all-gather.40
  741.0 45.1 all-gather.42
  798.2 128.7 all-gather.44
  929.2 50.2 all-gather.46
